TPU v7x, 32 devices: a whole 2x2x4 slice. The times are simulated.
32 devices in a mesh: replica: 8 (over y, x, core), tensor: 4 (over z).
Axes of the slice: x: 2, y: 2, z: 4, core: 2. Of those that a mesh axis runs over, the one named last changes fastest.
Arguments:
- inputs: bfloat16 [4096, 4096], P('replica', 'tensor'), may hold values from -6 to 6
- out_grad: bfloat16 [4096, 2560], P(('replica', 'tensor')), may hold values from -6 to 6
- weight: bfloat16 [4096, 2560], P('tensor'), may hold values from -0.09375 to 0.09375
- momentum: bfloat16 [8, 4096, 2560], P('replica', 'tensor'), may hold values from -6 to 6
- selected: int32 [2560, 64], P('tensor'), may hold values from 0 to 4095, as said below
Outputs:
- input_grad: bfloat16 [4096, 4096], P('replica', 'tensor')
- new_momentum: bfloat16 [8, 4096, 2560], P('replica', 'tensor')
- update: bfloat16 [4096, 2560], P('tensor')
Inputs may be any that keep to these rules, and one draw needn't show every extreme that they name: `selected`: each row holds 64 different frequency numbers u * 64 + v of one block; the same selection holds for every replica.
All inputs are finite; a program needn't handle non-finite values.
Results may differ from a plain program's by a relative error of at most 0.001.
Values may be sent and summed in bfloat16 or wider, within the bound.
A program may use at most 192 MiB of HBM per device.

v0:
```python
import math

import jax
import jax.numpy as jnp
from jax import lax
from jax.sharding import PartitionSpec as P

BLK = 64
TOPK = 64


HIGH = lax.Precision.HIGHEST


def basis_rows(freq):
    place = jnp.arange(BLK, dtype=jnp.float32)
    angle = math.pi * (2.0 * place + 1.0) / (2.0 * BLK)
    fvals = freq.astype(jnp.float32)[..., None]
    table = jnp.cos(fvals * angle) * math.sqrt(2.0 / BLK)
    return jnp.where(fvals == 0.0, math.sqrt(1.0 / BLK), table)


def body(inputs, out_grad, weight, momentum, selected):
    rows, cols = weight.shape
    tokens = inputs.shape[0]
    scale = 1.0 / math.sqrt(tokens)
    gathered = lax.all_gather(out_grad, "tensor", axis=0, tiled=True)
    wgrad = lax.dot_general(
        inputs, gathered, (((0,), (0,)), ((), ())), preferred_element_type=jnp.float32
    )
    dacts = lax.dot_general(
        gathered, weight, (((1,), (1,)), ((), ())), preferred_element_type=jnp.float32
    )
    wgrad = wgrad * scale
    accum = 0.999 * momentum[0].astype(jnp.float32) + wgrad
    block_rows_n = rows // BLK
    block_cols_n = cols // BLK
    row_basis = basis_rows(selected // BLK).reshape(block_rows_n, block_cols_n, TOPK, BLK)
    col_basis = basis_rows(selected % BLK).reshape(block_rows_n, block_cols_n, TOPK, BLK)
    split = accum.reshape(block_rows_n, BLK, block_cols_n, BLK)
    proj = jnp.einsum("rcki,ricj->rckj", row_basis, split, precision=HIGH)
    picked = jnp.sum(proj * col_basis, axis=-1).reshape(block_rows_n * block_cols_n, TOPK)
    mean_sent = lax.psum(picked, "replica") / lax.axis_size("replica")
    both = jnp.stack([picked, mean_sent], axis=0).reshape(2, block_rows_n, block_cols_n, TOPK)
    weighted = col_basis[None] * both[..., None]
    blocks = jnp.einsum("rcki,nrckj->nricj", row_basis, weighted, precision=HIGH)
    blocks = blocks.reshape(2, rows, cols)
    fresh = accum - blocks[0]
    update = BLK / math.sqrt(TOPK) * blocks[1]
    return (
        dacts.astype(jnp.bfloat16),
        fresh.astype(jnp.bfloat16)[None],
        update.astype(jnp.bfloat16),
    )


def solution(mesh):
    return jax.shard_map(
        body,
        mesh=mesh,
        in_specs=(
            P("replica", "tensor"),
            P(("replica", "tensor"), None),
            P("tensor", None),
            P("replica", "tensor", None),
            P("tensor", None),
        ),
        out_specs=(P("replica", "tensor"), P("replica", "tensor", None), P("tensor", None)),
        check_vma=False,
    )
```

profile of v0, /device:TPU:0, one launch (start us, length us, event | category | flops | bytes accessed | tf_op | source)
XLA Modules:
  0.0 556.5 jit_solution(5541792994715899460)
XLA Ops:
  7.2 0.0 copy-start
  7.2 0.0 all-gather.2.cloned.1.call-start
  7.2 0.7 all-gather.2.cloned.1.call-update
  7.9 0.0 all-reduce.2.cloned.1.call-start
  8.0 1.1 copy.16
  9.1 0.4 broadcast_compare_fusion
  9.5 72.0 %multiply_select_fusion.3 = f32[16,40,64,64]{2,3,1,0:T(8,128)} fusion(f32[64]{0:T(128)S(1)} %add_multiply_fusion, f32[16,40,64]{2,1,0:T(8,128)S(1)} %bitcast.40, pred[16,40,64]{2,1,0:T(8,128)(4,1)S(1)} %bitcast.44), kind=kLoop, calls=%fused_computation.11 | loop fusion | flops 7864320 | bytes 10690816 | tf_op jit(solution)/shard_map/jit(_where)/select_n | solution.py:20
  81.4 0.0 all-gather.2.cloned.1.call-done
  81.4 0.0 copy-done
  81.4 8.5 %bitcast_add_fusion = f32[1024,2560]{1,0:T(8,128)} fusion(bf16[1,1024,2560]{2,1,0:T(8,128)(2,1)} %param.8, bf16[512,1024]{1,0:T(8,128)(2,1)S(1)} %copy-done, bf16[512,2560]{1,0:T(8,128)(2,1)} %all-gather.2.cloned.1.call-done), kind=kOutput, calls=%fused_computation.13 | convolution fusion | flops 2694840320 | bytes 19398656 | tf_op jit(solution)/shard_map/dot_general | solution.py:28
  89.9 15.7 %reshape.55 = f32[16,64,40,64]{3,2,1,0:T(8,128)} reshape(f32[1024,2560]{1,0:T(8,128)} %bitcast_add_fusion) | data formatting | bytes 20971520 | tf_op jit(solution)/shard_map/reshape | solution.py:40
  105.6 162.7 %multiply_reduce_fusion = f32[16,40,64]{2,1,0:T(8,128)} fusion(f32[64]{0:T(128)S(1)} %add_multiply_fusion, f32[16,40,64]{2,1,0:T(8,128)S(1)} %bitcast.41, pred[16,40,64]{2,1,0:T(8,128)(4,1)S(1)} %bitcast.45, f32[16,64,40,64]{3,2,1,0:T(8,128)} %reshape.55, f32[16,40,64]{2,1,0:T(8,128)S(1)} %bitcast.35, pred[16,40,64]{2,1,0:T(8,128)(4,1)S(1)} %bitcast.42), kind=kOutput, calls=%fused_computation.8 | convolution fusion | flops 2034196480 | bytes 11059456 | tf_op jit(solution)/shard_map/rcki,ricj->rckj/dot_general | solution.py:41
  268.3 0.0 all-reduce.2.cloned.1.call-update
  268.3 7.2 %convolution_convert_fusion = bf16[512,1024]{1,0:T(8,128)(2,1)} fusion(bf16[512,2560]{1,0:T(8,128)(2,1)} %all-gather.2.cloned.1.call-done, bf16[1024,2560]{1,0:T(8,128)(2,1)} %param.7), kind=kOutput, calls=%fused_computation.26 | convolution fusion | flops 2684878848 | bytes 8912896 | tf_op jit(solution)/shard_map/dot_general | solution.py:31
  275.5 49.9 %all-reduce.2.cloned.1.call-done = f32[640,64]{1,0:T(8,128)} async-done(((f32[640,64]{1,0:T(8,128)}), f32[640,64]{1,0:T(8,128)}) %all-reduce.2.cloned.1.call-update) | async-done | bytes 163856 | tf_op jit(solution)/shard_map/psum | solution.py:43
  325.3 1.0 broadcast_multiply_fusion
  326.3 1.7 maximum_bitcast_fusion
  328.0 114.4 %fusion.8 = f32[2,16,64,40,64]{2,4,0,3,1:T(8,128)} fusion(f32[2,16,40,64]{3,0,2,1:T(2,128)S(1)} %maximum_bitcast_fusion, f32[16,40,64,64]{2,3,1,0:T(8,128)} %multiply_select_fusion.3, f32[16,40,64]{2,1,0:T(8,128)S(1)} %bitcast.36, f32[64]{0:T(128)S(1)} %add_multiply_fusion, pred[16,40,64]{2,1,0:T(8,128)(4,1)S(1)} %bitcast.43), kind=kOutput, calls=%fused_computation.12 | convolution fusion | flops 4039639040 | bytes 31990016 | tf_op jit(solution)/shard_map/rcki,nrckj->nricj/dot_general | solution.py:46
  442.4 26.7 %fusion.2 = (bf16[1,16,64,40,64]{2,4,0,3,1:T(8,128)(2,1)}, f32[1,16,64,40,64]{2,4,0,3,1:T(8,128)}) fusion(f32[2,16,64,40,64]{2,4,0,3,1:T(8,128)} %fusion.8), kind=kLoop, calls=%fused_computation.3 | loop fusion | flops 5242880 | bytes 36700160 | tf_op jit(solution)/shard_map/convert_element_type | solution.py:53
  469.1 15.5 %copy.24 = bf16[1,16,64,40,64]{4,3,2,1,0:T(8,128)(2,1)} copy(bf16[1,16,64,40,64]{2,4,0,3,1:T(8,128)(2,1)} %get-tuple-element.7) | data formatting | bytes 10485760 | tf_op jit(solution)/shard_map/convert_element_type | solution.py:53
  484.6 14.4 %convert_element_type.28 = bf16[1024,2560]{1,0:T(8,128)(2,1)} reshape(bf16[1,16,64,40,64]{4,3,2,1,0:T(8,128)(2,1)} %copy.24) | data formatting | bytes 10485760 | tf_op jit(solution)/shard_map/convert_element_type | solution.py:53
  499.0 21.8 %copy.23 = f32[1,16,64,40,64]{4,3,2,1,0:T(8,128)} copy(f32[1,16,64,40,64]{2,4,0,3,1:T(8,128)} %get-tuple-element.8) | data formatting | bytes 20971520 | tf_op jit(solution)/shard_map/slice | solution.py:48
  520.8 0.0 copy-start.1
  520.8 17.8 %squeeze.2 = f32[1024,2560]{1,0:T(8,128)} reshape(f32[1,16,64,40,64]{4,3,2,1,0:T(8,128)} %copy.23) | data formatting | bytes 20971520 | tf_op jit(solution)/shard_map/squeeze | solution.py:48
  538.6 11.1 %fusion.23 = bf16[1,1024,2560]{2,1,0:T(8,128)(2,1)} fusion(f32[1024,2560]{1,0:T(8,128)} %bitcast_add_fusion, f32[1024,2560]{1,0:T(8,128)} %squeeze.2), kind=kLoop, calls=%fused_computation.25 | loop fusion | flops 5242880 | bytes 26214400 | tf_op jit(solution)/shard_map/broadcast_in_dim | solution.py:52
  549.7 0.0 copy-done.1
  (1 shorter events, 0.0 us)
Async XLA Ops:
  7.2 74.3 %copy-start = (bf16[512,1024]{1,0:T(8,128)(2,1)S(1)}, bf16[512,1024]{1,0:T(8,128)(2,1)}, u32[]{:S(2)}) copy-start(bf16[512,1024]{1,0:T(8,128)(2,1)} %param.5) | copy-start | bytes 3145732
  7.2 74.2 %all-gather.2.cloned.1.call-start = ((), (), s32[]{:S(2)}) async-start(), calls=%async_computation | async-start | bytes 3276800 | tf_op jit(solution)/shard_map/all_gather | solution.py:27
  7.9 317.4 %all-reduce.2.cloned.1.call-start = ((), (), s32[]{:S(2)}) async-start(), calls=%async_computation.1 | async-start | bytes 655360 | tf_op jit(solution)/shard_map/psum | solution.py:43
  520.8 28.9 %copy-start.1 = (bf16[512,1024]{1,0:T(8,128)(2,1)S(1)}, bf16[512,1024]{1,0:T(8,128)(2,1)}, u32[]{:S(2)}) copy-start(bf16[512,1024]{1,0:T(8,128)(2,1)} %param.5) | copy-start | bytes 3145732
Sparse Core Ops, SparseCore 0:
  9.6 57.4 all-gather.1
  268.4 56.8 all-reduce.1
where the time goes:
time: 559 us; the launch traced here: 557 us
  matrix products  293 us (52%)
  other arithmetic  113 us (20%)
  local copies, waits for them, and re-layouts  86.2 us (15%)
  waiting for transfers between devices  50.6 us (9%)
  between operations  14.1 us (3%)
    dot_general x1, matrix products, body(): proj = jnp.einsum('rcki,ricj->rckj', row_basis, split, precision=HIGH)  163 us
    dot_general x1, matrix products, body(): jnp.einsum('rcki,nrckj->nricj', row_basis, weighted, precision=HIGH)  114 us
    select_n x1, other arithmetic, basis_rows(): return jnp.where(fvals == 0.0, math.sqrt(1.0 / BLK), table)  72 us
    psum x1, waiting for transfers between devices, body(): mean_sent = lax.psum(picked, 'replica') / lax.axis_size('replica')  49.9 us
    convert_element_type x2, local copies, waits for them, and re-layouts, body(): update.astype(jnp.bfloat16)  29.8 us
    convert_element_type x1, other arithmetic, body(): update.astype(jnp.bfloat16)  26.7 us
    slice x1, local copies, waits for them, and re-layouts, body(): fresh = accum - blocks[0]  21.8 us
    squeeze x1, local copies, waits for them, and re-layouts, body(): fresh = accum - blocks[0]  17.8 us
  transfers between devices with their start and end apart: 2, of which 1 were waited for; matrix products, arithmetic and copies ran while one was open for 14% of the time, Pallas kernels for 0%

commit v1 on v0

v1 whole, which is shorter than its diff:
```python
import functools
import math

import jax
import jax.numpy as jnp
import numpy as np
from jax import lax
from jax.experimental import pallas as pl
from jax.experimental.pallas import tpu as pltpu
from jax.sharding import PartitionSpec as P

BLK = 64
TOPK = 64
LANES = 2 * BLK
WIDE = 256


def dct_table():
    place = np.arange(BLK)[:, None]
    freq = np.arange(BLK)[None, :]
    table = np.cos(math.pi * (2.0 * place + 1.0) * freq / (2.0 * BLK)) * math.sqrt(2.0 / BLK)
    table[:, 0] = math.sqrt(1.0 / BLK)
    return np.concatenate([table, table], axis=1).astype(np.float32)


def split(x):
    high = x.astype(jnp.bfloat16)
    low = (x - high.astype(jnp.float32)).astype(jnp.bfloat16)
    return high, low


def bases(picks, table):
    rows_at = jnp.broadcast_to(lax.shift_right_logical(picks, 6), (BLK, LANES))
    cols_at = jnp.broadcast_to(picks & (BLK - 1), (BLK, LANES))
    row_basis = jnp.take_along_axis(table, rows_at, axis=1)
    col_basis = jnp.take_along_axis(table, cols_at, axis=1)
    first = lax.broadcasted_iota(jnp.int32, (BLK, LANES), 1) < BLK
    diagonal = jnp.concatenate(
        [jnp.where(first, col_basis, 0.0), jnp.where(first, 0.0, col_basis)], axis=0
    )
    return row_basis, split(diagonal)


def encode(block, row_basis, diagonal):
    high, low = split(block)
    dhigh, dlow = diagonal
    both = jnp.concatenate([dhigh, dlow], axis=1)
    part = jnp.dot(
        jnp.concatenate([high, low], axis=1),
        jnp.concatenate([both, both], axis=0),
        preferred_element_type=jnp.float32,
    )
    proj = part[:, :LANES] + part[:, LANES:]
    return jnp.sum(row_basis * proj, axis=0, keepdims=True)


def decode(values, row_basis, diagonal):
    high, low = split(row_basis * values)
    dhigh, dlow = diagonal
    both = jnp.concatenate([dhigh, dlow], axis=0)
    part = lax.dot_general(
        jnp.concatenate([high, low], axis=1),
        jnp.concatenate([both, both], axis=1),
        (((1,), (1,)), ((), ())),
        preferred_element_type=jnp.float32,
    )
    return part[:, :LANES] + part[:, LANES:]


def group_of(strips):
    return 8 if strips % 8 == 0 else strips


def momentum_kernel(scale, strips, x_ref, g_ref, m_ref, sel_ref, table_ref, fresh_ref, sent_ref, acc_ref):
    acc_ref[...] = (
        jnp.dot(x_ref[...], g_ref[...], preferred_element_type=jnp.float32) * scale
        + 0.999 * m_ref[...].astype(jnp.float32)
    )
    table = table_ref[...]

    some = group_of(strips)

    @pl.loop(0, strips // some)
    def _(group):
        near = pl.ds(pl.multiple_of(group * some, some), some)
        for pair in range(WIDE // LANES):
            lanes = pl.ds(pair * LANES, LANES)
            picks = sel_ref[0, near, lanes]
            found = []
            for one in range(some):
                at = pl.ds(pl.multiple_of((group * some + one) * BLK, BLK), BLK)
                row_basis, diagonal = bases(picks[one : one + 1], table)
                block = acc_ref[at, lanes]
                values = encode(block, row_basis, diagonal)
                found.append(values)
                fresh_ref[at, lanes] = (block - decode(values, row_basis, diagonal)).astype(jnp.bfloat16)
            sent_ref[0, near, lanes] = jnp.concatenate(found, axis=0)


def update_kernel(strips, mean_ref, sel_ref, table_ref, update_ref):
    table = table_ref[...]

    some = group_of(strips)

    @pl.loop(0, strips // some)
    def _(group):
        near = pl.ds(pl.multiple_of(group * some, some), some)
        for pair in range(WIDE // LANES):
            lanes = pl.ds(pair * LANES, LANES)
            picks = sel_ref[0, near, lanes]
            means = mean_ref[0, near, lanes] * (BLK / math.sqrt(TOPK))
            for one in range(some):
                at = pl.ds(pl.multiple_of((group * some + one) * BLK, BLK), BLK)
                row_basis, diagonal = bases(picks[one : one + 1], table)
                update_ref[at, lanes] = decode(means[one : one + 1], row_basis, diagonal).astype(jnp.bfloat16)


def body(inputs, out_grad, weight, momentum, selected):
    rows, cols = weight.shape
    tokens = inputs.shape[0]
    scale = 1.0 / math.sqrt(tokens)
    strips, steps = rows // BLK, cols // WIDE
    table = jnp.asarray(dct_table())
    gathered = lax.all_gather(out_grad, "tensor", axis=0, tiled=True)
    turned = inputs.T
    picks = selected.reshape(strips, steps, WIDE).swapaxes(0, 1)

    small = pl.BlockSpec((1, strips, WIDE), lambda c: (c, 0, 0))
    whole_table = pl.BlockSpec((BLK, LANES), lambda c: (0, 0))
    tall = pl.BlockSpec((rows, WIDE), lambda c: (0, c))
    fresh, sent = pl.pallas_call(
        functools.partial(momentum_kernel, scale, strips),
        grid=(steps,),
        out_shape=(
            jax.ShapeDtypeStruct((rows, cols), jnp.bfloat16),
            jax.ShapeDtypeStruct((steps, strips, WIDE), jnp.float32),
        ),
        in_specs=[
            pl.BlockSpec((rows, tokens), lambda c: (0, 0)),
            pl.BlockSpec((tokens, WIDE), lambda c: (0, c)),
            tall,
            small,
            whole_table,
        ],
        out_specs=(tall, small),
        scratch_shapes=[pltpu.VMEM((rows, WIDE), jnp.float32)],
        cost_estimate=pl.CostEstimate(
            flops=2 * rows * cols * (tokens + 512), bytes_accessed=8 * rows * cols, transcendentals=0
        ),
        name="momentum_step",
    )(turned, gathered, momentum[0], picks, table)
    mean_sent = lax.psum(sent, "replica") / lax.axis_size("replica")
    dacts = lax.dot_general(
        gathered, weight, (((1,), (1,)), ((), ())), preferred_element_type=jnp.float32
    ).astype(jnp.bfloat16)
    update = pl.pallas_call(
        functools.partial(update_kernel, strips),
        grid=(steps,),
        out_shape=jax.ShapeDtypeStruct((rows, cols), jnp.bfloat16),
        in_specs=[small, small, whole_table],
        out_specs=tall,
        cost_estimate=pl.CostEstimate(
            flops=2 * rows * cols * 256, bytes_accessed=2 * rows * cols, transcendentals=0
        ),
        name="update_step",
    )(mean_sent, picks, table)
    return dacts, fresh[None], update


def solution(mesh):
    return jax.shard_map(
        body,
        mesh=mesh,
        in_specs=(
            P("replica", "tensor"),
            P(("replica", "tensor"), None),
            P("tensor", None),
            P("replica", "tensor", None),
            P("tensor", None),
        ),
        out_specs=(P("replica", "tensor"), P("replica", "tensor", None), P("tensor", None)),
        check_vma=False,
    )
```

time: 559 us -> 189 us (0.34)
  matrix products: 293 us -> 6.36 us
  other arithmetic: 113 us -> 1.59 us
  local copies, waits for them, and re-layouts: 86.2 us -> 4.27 us
  Pallas kernels: 0 us -> 62.3 us
  waiting for transfers between devices: 50.6 us -> 100 us
    dot_general x3 -> x0, matrix products: 286 us -> none  [the longest x1 163 us: body(): proj = jnp.einsum('rcki,ricj->rckj', row_basis, split, precision=HIGH)]
    select_n x1 -> x0, other arithmetic: 72 us -> none  [basis_rows(): return jnp.where(fvals == 0.0, math.sqrt(1.0 / BLK), table)]
    pallas_call x0 -> x2, Pallas kernels: none -> 62.3 us  [the longest x1 43.9 us: body(): pl.pallas_call(functools.partial(momentum_kernel, scale, strips), grid=(s...]
    all_gather x1, waiting for transfers between devices: 0.01 us -> 54.8 us  [body(): gathered = lax.all_gather(out_grad, 'tensor', axis=0, tiled=True)]
    convert_element_type x2 -> x0, local copies, waits for them, and re-layouts: 29.8 us -> none  [body(): update.astype(jnp.bfloat16)]
    convert_element_type x1 -> x0, other arithmetic: 26.7 us -> none  [body(): update.astype(jnp.bfloat16)]
    slice x1 -> x0, local copies, waits for them, and re-layouts: 21.8 us -> none  [body(): fresh = accum - blocks[0]]
    squeeze x1 -> x0, local copies, waits for them, and re-layouts: 17.8 us -> none  [body(): fresh = accum - blocks[0]]
  transfers between devices with their start and end apart: 2 -> 2, of which waited for: 1 -> 2; matrix products, arithmetic and copies ran while one was open for 14% -> 6% of each run, Pallas kernels for 0% -> 0%
where the time goes in v1:
time: 189 us
  waiting for transfers between devices  100 us (53%)
  Pallas kernels  62.3 us (33%)
  between operations  14.1 us (7%)
  matrix products  6.36 us (3%)
  local copies, waits for them, and re-layouts  4.27 us (2%)
    all_gather x1, waiting for transfers between devices, body(): gathered = lax.all_gather(out_grad, 'tensor', axis=0, tiled=True)  54.8 us
    psum x1, waiting for transfers between devices, body(): mean_sent = lax.psum(sent, 'replica') / lax.axis_size('replica')  44.9 us
    pallas_call x1, Pallas kernels, body(): pl.pallas_call(functools.partial(momentum_kernel, scale, strips), grid=(s...  43.9 us
    pallas_call x1, Pallas kernels, body(): pl.pallas_call(functools.partial(update_kernel, strips), grid=(steps,), o...  18.4 us
    dot_general x1, matrix products, body(): lax.dot_general(gathered, weight, (((1,), (1,)), ((), ())), preferred_ele...  6.36 us
  transfers between devices with their start and end apart: 2, of which 2 were waited for; matrix products, arithmetic and copies ran while one was open for 6% of the time, Pallas kernels for 0%

profile of v1, /device:TPU:0, one launch (start us, length us, event | category | flops | bytes accessed | tf_op | source)
XLA Modules:
  0.0 189.0 jit_solution(2337661111609892195)
XLA Ops:
  7.2 0.0 all-gather.2.cloned.1.call-start
  7.2 0.7 all-gather.2.cloned.1.call-update
  7.9 0.0 all-reduce.2.cloned.1.call-start
  7.9 1.1 copy.11
  9.0 0.1 reshape.9
  9.2 0.8 copy.14
  9.9 2.3 %copy.10 = bf16[512,1024]{0,1:T(8,128)(2,1)} copy(bf16[512,1024]{1,0:T(8,128)(2,1)} %param.6) | data formatting | bytes 2097152 | tf_op args[0]
  12.2 54.8 %all-gather.2.cloned.1.call-done.g_ref = bf16[512,2560]{1,0:T(8,128)(2,1)} async-done(((bf16[128,2560]{1,0:T(8,128)(2,1)}), bf16[512,2560]{1,0:T(8,128)(2,1)}) %all-gather.2.cloned.1.call-update) | async-done | bytes 2621456 | tf_op jit(solution)/shard_map/all_gather | solution.py:124
  67.0 0.0 copy-start
  67.0 43.9 %momentum_step.1 = (bf16[1024,2560]{1,0:T(8,128)(2,1)}, f32[10,16,256]{2,1,0:T(8,128)}) custom-call(bf16[1024,512]{1,0:T(8,128)(2,1)} %bitcast.8, bf16[512,2560]{1,0:T(8,128)(2,1)} %all-gather.2.cloned.1.call-done.g_ref, bf16[1024,2560]{1,0:T(8,128)(2,1)} %bitcast.11, s32[10,16,256]{2,1,0:T(8,128)} %bitcast.9, f32[64,128]{1,0:T(8,128)} %constant.5.clone.table_ref), custom_call_target="tpu_custom_call" | custom-call | flops 5368709120 | bytes 20971520 | tf_op jit(solution)/shard_map/momentum_step/pallas_call | solution.py:131
  110.9 0.0 all-reduce.2.cloned.1.call-update
  110.9 0.0 copy-done
  110.9 6.4 %convolution_convert_fusion = bf16[512,1024]{1,0:T(8,128)(2,1)} fusion(bf16[512,2560]{1,0:T(8,128)(2,1)S(1)} %copy-done, bf16[1024,2560]{1,0:T(8,128)(2,1)} %param.8), kind=kOutput, calls=%fused_computation | convolution fusion | flops 2684878848 | bytes 8912896 | tf_op jit(solution)/shard_map/dot_general | solution.py:153
  117.3 44.9 %all-reduce.2.cloned.1.call-done = f32[10,16,256]{2,1,0:T(8,128)} async-done(((f32[10,16,256]{2,1,0:T(8,128)}), f32[10,16,256]{2,1,0:T(8,128)}) %all-reduce.2.cloned.1.call-update) | async-done | bytes 163856 | tf_op jit(solution)/shard_map/psum | solution.py:152
  162.2 1.6 broadcast_multiply_fusion.mean_ref
  163.8 18.4 %update_step.1 = bf16[1024,2560]{1,0:T(8,128)(2,1)} custom-call(f32[10,16,256]{2,1,0:T(8,128)} %broadcast_multiply_fusion.mean_ref, s32[10,16,256]{2,1,0:T(8,128)} %bitcast.10, f32[64,128]{1,0:T(8,128)} %constant.5.clone.table_ref), custom_call_target="tpu_custom_call" | custom-call | flops 1342177280 | bytes 5242880 | tf_op jit(solution)/shard_map/update_step/pallas_call | solution.py:156
Async XLA Ops:
  7.2 59.9 %all-gather.2.cloned.1.call-start = ((), (), s32[]{:S(2)}) async-start(), calls=%async_computation | async-start | bytes 3276800 | tf_op jit(solution)/shard_map/all_gather | solution.py:124
  7.9 154.3 %all-reduce.2.cloned.1.call-start = ((), (), s32[]{:S(2)}) async-start(), calls=%async_computation.1 | async-start | bytes 327680 | tf_op jit(solution)/shard_map/psum | solution.py:152
  67.0 43.9 %copy-start = (bf16[512,2560]{1,0:T(8,128)(2,1)S(1)}, bf16[512,2560]{1,0:T(8,128)(2,1)}, u32[]{:S(2)}) copy-start(bf16[512,2560]{1,0:T(8,128)(2,1)} %all-gather.2.cloned.1.call-done.g_ref) | copy-start | bytes 7864324
Sparse Core Ops, SparseCore 0:
  9.5 57.4 all-gather.1
  111.0 51.0 all-reduce.1

commit v2 on v1

--- a/solution.py
+++ b/solution.py
@@ -44,27 +44,25 @@
 def encode(block, row_basis, diagonal):
     high, low = split(block)
     dhigh, dlow = diagonal
-    both = jnp.concatenate([dhigh, dlow], axis=1)
     part = jnp.dot(
-        jnp.concatenate([high, low], axis=1),
-        jnp.concatenate([both, both], axis=0),
+        jnp.concatenate([high, low], axis=0),
+        jnp.concatenate([dhigh, dlow], axis=1),
         preferred_element_type=jnp.float32,
     )
-    proj = part[:, :LANES] + part[:, LANES:]
+    proj = part[:BLK, :LANES] + (part[:BLK, LANES:] + part[BLK:, :LANES])
     return jnp.sum(row_basis * proj, axis=0, keepdims=True)
 
 
 def decode(values, row_basis, diagonal):
     high, low = split(row_basis * values)
     dhigh, dlow = diagonal
-    both = jnp.concatenate([dhigh, dlow], axis=0)
     part = lax.dot_general(
-        jnp.concatenate([high, low], axis=1),
-        jnp.concatenate([both, both], axis=1),
+        jnp.concatenate([high, low], axis=0),
+        jnp.concatenate([dhigh, dlow], axis=0),
         (((1,), (1,)), ((), ())),
         preferred_element_type=jnp.float32,
     )
-    return part[:, :LANES] + part[:, LANES:]
+    return part[:BLK, :LANES] + (part[:BLK, LANES:] + part[BLK:, :LANES])
 
 
 def group_of(strips):
@@ -85,7 +83,7 @@
         near = pl.ds(pl.multiple_of(group * some, some), some)
         for pair in range(WIDE // LANES):
             lanes = pl.ds(pair * LANES, LANES)
-            picks = sel_ref[0, near, lanes]
+            picks = sel_ref[pair, near]
             found = []
             for one in range(some):
                 at = pl.ds(pl.multiple_of((group * some + one) * BLK, BLK), BLK)
@@ -94,7 +92,7 @@
                 values = encode(block, row_basis, diagonal)
                 found.append(values)
                 fresh_ref[at, lanes] = (block - decode(values, row_basis, diagonal)).astype(jnp.bfloat16)
-            sent_ref[0, near, lanes] = jnp.concatenate(found, axis=0)
+            sent_ref[pair, near] = jnp.concatenate(found, axis=0)
 
 
 def update_kernel(strips, mean_ref, sel_ref, table_ref, update_ref):
@@ -107,12 +105,127 @@
         near = pl.ds(pl.multiple_of(group * some, some), some)
         for pair in range(WIDE // LANES):
             lanes = pl.ds(pair * LANES, LANES)
-            picks = sel_ref[0, near, lanes]
-            means = mean_ref[0, near, lanes] * (BLK / math.sqrt(TOPK))
+            picks = sel_ref[pair, near]
+            means = mean_ref[pair, near] * (BLK / math.sqrt(TOPK))
             for one in range(some):
                 at = pl.ds(pl.multiple_of((group * some + one) * BLK, BLK), BLK)
                 row_basis, diagonal = bases(picks[one : one + 1], table)
                 update_ref[at, lanes] = decode(means[one : one + 1], row_basis, diagonal).astype(jnp.bfloat16)
+
+
+def greet(axis, n):
+    me = lax.axis_index(axis)
+    barrier = pltpu.get_barrier_semaphore()
+    for step in range(1, n):
+        pl.semaphore_signal(
+            barrier, inc=1, device_id={axis: lax.rem(me + step, n)}, device_id_type=pl.DeviceIdType.MESH
+        )
+    pl.semaphore_wait(barrier, n - 1)
+    return me
+
+
+def gather_kernel(axis, n, own_ref, all_ref, send_sem, recv_sem, own_sem):
+    me = greet(axis, n)
+    depth = own_ref.shape[0]
+    place = all_ref.at[pl.ds(pl.multiple_of(me * depth, depth), depth)]
+    copies = [
+        pltpu.make_async_remote_copy(
+            src_ref=own_ref,
+            dst_ref=place,
+            send_sem=send_sem.at[step],
+            recv_sem=recv_sem.at[step],
+            device_id={axis: lax.rem(me + step, n)},
+            device_id_type=pl.DeviceIdType.MESH,
+        )
+        for step in range(1, n)
+    ]
+    for copy in copies:
+        copy.start()
+    own = pltpu.make_async_copy(own_ref, place, own_sem)
+    own.start()
+    own.wait()
+    for copy in copies:
+        copy.wait()
+
+
+def mean_kernel(axis, n, sent_ref, mean_ref, parts, total, send_sem, recv_sem, back_sem, give_sem):
+    me = greet(axis, n)
+    scatter = []
+    spread = []
+    for step in range(1, n):
+        peer = lax.rem(me + step, n)
+        scatter.append(
+            pltpu.make_async_remote_copy(
+                src_ref=sent_ref.at[peer],
+                dst_ref=parts.at[step],
+                send_sem=send_sem.at[step],
+                recv_sem=recv_sem.at[step],
+                device_id={axis: peer},
+                device_id_type=pl.DeviceIdType.MESH,
+            )
+        )
+        spread.append(
+            pltpu.make_async_remote_copy(
+                src_ref=total,
+                dst_ref=mean_ref.at[me],
+                send_sem=back_sem.at[step],
+                recv_sem=give_sem.at[step],
+                device_id={axis: peer},
+                device_id_type=pl.DeviceIdType.MESH,
+            )
+        )
+    for copy in scatter:
+        copy.start()
+    value = sent_ref[me]
+    for step, copy in enumerate(scatter, 1):
+        copy.wait_recv()
+        value = value + parts[step]
+    total[...] = value / n
+    for copy in spread:
+        copy.start()
+    mean_ref[me] = total[...]
+    for copy in scatter:
+        copy.wait_send()
+    for copy in spread:
+        copy.wait()
+
+
+def gather_rows(array, axis):
+    n = lax.axis_size(axis)
+    depth, cols = array.shape
+    return pl.pallas_call(
+        functools.partial(gather_kernel, axis, n),
+        out_shape=jax.ShapeDtypeStruct((n * depth, cols), array.dtype),
+        in_specs=[pl.BlockSpec(memory_space=pltpu.VMEM)],
+        out_specs=pl.BlockSpec(memory_space=pl.ANY),
+        scratch_shapes=[
+            pltpu.SemaphoreType.DMA((n,)),
+            pltpu.SemaphoreType.DMA((n,)),
+            pltpu.SemaphoreType.DMA,
+        ],
+        compiler_params=pltpu.CompilerParams(collective_id=0, has_side_effects=True),
+        name="gather_rows",
+    )(array)
+
+
+def mean_over(array, axis):
+    n = lax.axis_size(axis)
+    lanes = array.shape[-1]
+    slices = array.reshape(n, -1, lanes)
+    mean = pl.pallas_call(
+        functools.partial(mean_kernel, axis, n),
+        out_shape=jax.ShapeDtypeStruct(slices.shape, jnp.float32),
+        in_specs=[pl.BlockSpec(memory_space=pltpu.VMEM)],
+        out_specs=pl.BlockSpec(memory_space=pltpu.VMEM),
+        scratch_shapes=[
+            pltpu.VMEM(slices.shape, jnp.float32),
+            pltpu.VMEM(slices.shape[1:], jnp.float32),
+        ]
+        + [pltpu.SemaphoreType.DMA((n,))] * 4,
+        compiler_params=pltpu.CompilerParams(collective_id=1, has_side_effects=True),
+        name="mean_over",
+    )(slices)
+    return mean.reshape(array.shape)
 
 
 def body(inputs, out_grad, weight, momentum, selected):
@@ -121,11 +234,11 @@
     scale = 1.0 / math.sqrt(tokens)
     strips, steps = rows // BLK, cols // WIDE
     table = jnp.asarray(dct_table())
-    gathered = lax.all_gather(out_grad, "tensor", axis=0, tiled=True)
+    gathered = gather_rows(out_grad, "tensor")
     turned = inputs.T
-    picks = selected.reshape(strips, steps, WIDE).swapaxes(0, 1)
-
-    small = pl.BlockSpec((1, strips, WIDE), lambda c: (c, 0, 0))
+    picks = selected.reshape(strips, cols // LANES, LANES).swapaxes(0, 1)
+
+    small = pl.BlockSpec((WIDE // LANES, strips, LANES), lambda c: (c, 0, 0))
     whole_table = pl.BlockSpec((BLK, LANES), lambda c: (0, 0))
     tall = pl.BlockSpec((rows, WIDE), lambda c: (0, c))
     fresh, sent = pl.pallas_call(
@@ -133,7 +246,7 @@
         grid=(steps,),
         out_shape=(
             jax.ShapeDtypeStruct((rows, cols), jnp.bfloat16),
-            jax.ShapeDtypeStruct((steps, strips, WIDE), jnp.float32),
+            jax.ShapeDtypeStruct((cols // LANES, strips, LANES), jnp.float32),
         ),
         in_specs=[
             pl.BlockSpec((rows, tokens), lambda c: (0, 0)),
@@ -149,7 +262,7 @@
         ),
         name="momentum_step",
     )(turned, gathered, momentum[0], picks, table)
-    mean_sent = lax.psum(sent, "replica") / lax.axis_size("replica")
+    mean_sent = mean_over(sent, "replica")
     dacts = lax.dot_general(
         gathered, weight, (((1,), (1,)), ((), ())), preferred_element_type=jnp.float32
     ).astype(jnp.bfloat16)

time: 189 us -> 129 us (0.68)
  the two profiles are of different devices: /device:TPU:0 before, /device:TPU:9 now
where the time goes in v2:
time: 129 us; the launch traced here: 128 us
  Pallas kernels  116 us (90%)
  matrix products  7.15 us (6%)
  local copies, waits for them, and re-layouts  4.16 us (3%)
    pallas_call x1, Pallas kernels, gather_rows(): pl.pallas_call(functools.partial(gather_kernel, axis, n), out_shape=jax.S...  61.1 us
    pallas_call x1, Pallas kernels, body(): pl.pallas_call(functools.partial(momentum_kernel, scale, strips), grid=(s...  25.5 us
    pallas_call x1, Pallas kernels, body(): pl.pallas_call(functools.partial(update_kernel, strips), grid=(steps,), o...  17.9 us
    pallas_call x1, Pallas kernels, mean_over(): pl.pallas_call(functools.partial(mean_kernel, axis, n), out_shape=jax.Sha...  11.8 us
    dot_general x1, matrix products, body(): lax.dot_general(gathered, weight, (((1,), (1,)), ((), ())), preferred_ele...  7.15 us
    unnamed x2, local copies, waits for them, and re-layouts  3.35 us

profile of v2, /device:TPU:9, one launch (start us, length us, event | category | flops | bytes accessed | tf_op | source)
XLA Modules:
  0.0 128.4 jit_solution(1915699891426091237)
XLA Ops:
  0.6 1.1 copy.11
  1.7 0.1 reshape.15
  1.8 0.7 copy.14
  2.5 2.3 %copy.10 = bf16[512,1024]{0,1:T(8,128)(2,1)} copy(bf16[512,1024]{1,0:T(8,128)(2,1)} %param.6) | data formatting | bytes 2097152 | tf_op args[0]
  4.8 61.1 %gather_rows.1.g_ref = bf16[512,2560]{1,0:T(8,128)(2,1)} custom-call(bf16[128,2560]{1,0:T(8,128)(2,1)} %own_ref.1), custom_call_target="tpu_custom_call" | custom-call | tf_op jit(solution)/shard_map/gather_rows/pallas_call | solution.py:196
  65.9 7.2 %convolution_convert_fusion = bf16[512,1024]{1,0:T(8,128)(2,1)} fusion(bf16[512,2560]{1,0:T(8,128)(2,1)} %gather_rows.1.g_ref, bf16[1024,2560]{1,0:T(8,128)(2,1)} %param.8), kind=kOutput, calls=%fused_computation | convolution fusion | flops 2684878848 | bytes 8912896 | tf_op jit(solution)/shard_map/dot_general | solution.py:266
  73.1 25.5 %momentum_step.1 = (bf16[1024,2560]{1,0:T(8,128)(2,1)}, f32[20,16,128]{2,1,0:T(8,128)}) custom-call(bf16[1024,512]{1,0:T(8,128)(2,1)} %bitcast.10, bf16[512,2560]{1,0:T(8,128)(2,1)} %gather_rows.1.g_ref, bf16[1024,2560]{1,0:T(8,128)(2,1)} %bitcast.15, s32[20,16,128]{2,1,0:T(8,128)} %bitcast.11, f32[64,128]{1,0:T(8,128)} %constant.2.clone.table_ref), custom_call_target="tpu_custom_call" | custom-call | flops 5368709120 | bytes 20971520 | tf_op jit(solution)/shard_map/momentum_step/pallas_call | solution.py:244
  98.6 11.8 %mean_over.1 = f32[8,40,128]{2,1,0:T(8,128)} custom-call(f32[8,40,128]{2,1,0:T(8,128)} %bitcast.14), custom_call_target="tpu_custom_call" | custom-call | tf_op jit(solution)/shard_map/mean_over/pallas_call | solution.py:215
  110.5 17.9 %update_step.1 = bf16[1024,2560]{1,0:T(8,128)(2,1)} custom-call(f32[20,16,128]{2,1,0:T(8,128)} %bitcast.13, s32[20,16,128]{2,1,0:T(8,128)} %bitcast.12, f32[64,128]{1,0:T(8,128)} %constant.2.clone.table_ref), custom_call_target="tpu_custom_call" | custom-call | flops 1342177280 | bytes 5242880 | tf_op jit(solution)/shard_map/update_step/pallas_call | solution.py:269

commit v3 on v2

--- a/solution.py
+++ b/solution.py
@@ -13,6 +13,7 @@
 TOPK = 64
 LANES = 2 * BLK
 WIDE = 256
+PIECES = 2
 
 
 def dct_table():
@@ -125,27 +126,45 @@
 
 
 def gather_kernel(axis, n, own_ref, all_ref, send_sem, recv_sem, own_sem):
-    me = greet(axis, n)
-    depth = own_ref.shape[0]
-    place = all_ref.at[pl.ds(pl.multiple_of(me * depth, depth), depth)]
-    copies = [
-        pltpu.make_async_remote_copy(
-            src_ref=own_ref,
-            dst_ref=place,
-            send_sem=send_sem.at[step],
-            recv_sem=recv_sem.at[step],
-            device_id={axis: lax.rem(me + step, n)},
+    me = lax.axis_index(axis)
+    right, left = lax.rem(me + 1, n), lax.rem(me + n - 1, n)
+    barrier = pltpu.get_barrier_semaphore()
+    for peer in (left, right):
+        pl.semaphore_signal(barrier, inc=1, device_id={axis: peer}, device_id_type=pl.DeviceIdType.MESH)
+    pl.semaphore_wait(barrier, 2)
+    depth, cols = own_ref.shape
+    width = cols // (2 * PIECES)
+
+    def rows_of(owner):
+        return pl.ds(pl.multiple_of(owner * depth, depth), depth)
+
+    def hop(step, piece, way):
+        owner = lax.rem(me + n - step, n) if way == 0 else lax.rem(me + step, n)
+        lanes = pl.ds((way * PIECES + piece) * width, width)
+        there = all_ref.at[rows_of(owner), lanes]
+        return pltpu.make_async_remote_copy(
+            src_ref=own_ref.at[:, lanes] if step == 0 else there,
+            dst_ref=there,
+            send_sem=send_sem.at[step, way * PIECES + piece],
+            recv_sem=recv_sem.at[step, way * PIECES + piece],
+            device_id={axis: right if way == 0 else left},
             device_id_type=pl.DeviceIdType.MESH,
         )
-        for step in range(1, n)
-    ]
-    for copy in copies:
+
+    hops = [[hop(step, piece, way) for piece in range(PIECES) for way in range(2)] for step in range(n - 1)]
+    for copy in hops[0]:
         copy.start()
-    own = pltpu.make_async_copy(own_ref, place, own_sem)
+    own = pltpu.make_async_copy(own_ref, all_ref.at[rows_of(me)], own_sem)
     own.start()
+    for step in range(n - 1):
+        for at, copy in enumerate(hops[step]):
+            copy.wait_recv()
+            if step + 1 < n - 1:
+                hops[step + 1][at].start()
     own.wait()
-    for copy in copies:
-        copy.wait()
+    for some in hops:
+        for copy in some:
+            copy.wait_send()
 
 
 def mean_kernel(axis, n, sent_ref, mean_ref, parts, total, send_sem, recv_sem, back_sem, give_sem):
@@ -199,8 +218,8 @@
         in_specs=[pl.BlockSpec(memory_space=pltpu.VMEM)],
         out_specs=pl.BlockSpec(memory_space=pl.ANY),
         scratch_shapes=[
-            pltpu.SemaphoreType.DMA((n,)),
-            pltpu.SemaphoreType.DMA((n,)),
+            pltpu.SemaphoreType.DMA((n - 1, 2 * PIECES)),
+            pltpu.SemaphoreType.DMA((n - 1, 2 * PIECES)),
             pltpu.SemaphoreType.DMA,
         ],
         compiler_params=pltpu.CompilerParams(collective_id=0, has_side_effects=True),

time: 129 us -> 116 us (0.90)
  the two profiles are of different devices: /device:TPU:9 before, /device:TPU:0 now
where the time goes in v3:
time: 116 us
  Pallas kernels  104 us (90%)
  matrix products  7.15 us (6%)
  local copies, waits for them, and re-layouts  4.16 us (4%)
    pallas_call x1, Pallas kernels, gather_rows(): pl.pallas_call(functools.partial(gather_kernel, axis, n), out_shape=jax.S...  48.8 us
    pallas_call x1, Pallas kernels, body(): pl.pallas_call(functools.partial(momentum_kernel, scale, strips), grid=(s...  25.6 us
    pallas_call x1, Pallas kernels, body(): pl.pallas_call(functools.partial(update_kernel, strips), grid=(steps,), o...  17.9 us
    pallas_call x1, Pallas kernels, mean_over(): pl.pallas_call(functools.partial(mean_kernel, axis, n), out_shape=jax.Sha...  11.7 us
    dot_general x1, matrix products, body(): lax.dot_general(gathered, weight, (((1,), (1,)), ((), ())), preferred_ele...  7.15 us
    unnamed x2, local copies, waits for them, and re-layouts  3.35 us

profile of v3, /device:TPU:0, one launch (start us, length us, event | category | flops | bytes accessed | tf_op | source)
XLA Modules:
  0.0 116.0 jit_solution(74832462493805926)
XLA Ops:
  0.6 1.1 copy.11
  1.7 0.1 reshape.15
  1.8 0.7 copy.14
  2.5 2.3 %copy.10 = bf16[512,1024]{0,1:T(8,128)(2,1)} copy(bf16[512,1024]{1,0:T(8,128)(2,1)} %param.6) | data formatting | bytes 2097152 | tf_op args[0]
  4.8 48.8 %gather_rows.1.g_ref = bf16[512,2560]{1,0:T(8,128)(2,1)} custom-call(bf16[128,2560]{1,0:T(8,128)(2,1)} %own_ref.1), custom_call_target="tpu_custom_call" | custom-call | tf_op jit(solution)/shard_map/gather_rows/pallas_call | solution.py:215
  53.6 7.2 %convolution_convert_fusion = bf16[512,1024]{1,0:T(8,128)(2,1)} fusion(bf16[512,2560]{1,0:T(8,128)(2,1)} %gather_rows.1.g_ref, bf16[1024,2560]{1,0:T(8,128)(2,1)} %param.8), kind=kOutput, calls=%fused_computation | convolution fusion | flops 2684878848 | bytes 8912896 | tf_op jit(solution)/shard_map/dot_general | solution.py:285
  60.8 25.6 %momentum_step.1 = (bf16[1024,2560]{1,0:T(8,128)(2,1)}, f32[20,16,128]{2,1,0:T(8,128)}) custom-call(bf16[1024,512]{1,0:T(8,128)(2,1)} %bitcast.10, bf16[512,2560]{1,0:T(8,128)(2,1)} %gather_rows.1.g_ref, bf16[1024,2560]{1,0:T(8,128)(2,1)} %bitcast.15, s32[20,16,128]{2,1,0:T(8,128)} %bitcast.11, f32[64,128]{1,0:T(8,128)} %constant.2.clone.table_ref), custom_call_target="tpu_custom_call" | custom-call | flops 5368709120 | bytes 20971520 | tf_op jit(solution)/shard_map/momentum_step/pallas_call | solution.py:263
  86.3 11.7 %mean_over.1 = f32[8,40,128]{2,1,0:T(8,128)} custom-call(f32[8,40,128]{2,1,0:T(8,128)} %bitcast.14), custom_call_target="tpu_custom_call" | custom-call | tf_op jit(solution)/shard_map/mean_over/pallas_call | solution.py:234
  98.0 17.9 %update_step.1 = bf16[1024,2560]{1,0:T(8,128)(2,1)} custom-call(f32[20,16,128]{2,1,0:T(8,128)} %bitcast.13, s32[20,16,128]{2,1,0:T(8,128)} %bitcast.12, f32[64,128]{1,0:T(8,128)} %constant.2.clone.table_ref), custom_call_target="tpu_custom_call" | custom-call | flops 1342177280 | bytes 5242880 | tf_op jit(solution)/shard_map/update_step/pallas_call | solution.py:288

commit v4 on v2

--- a/solution.py
+++ b/solution.py
@@ -13,6 +13,7 @@
 TOPK = 64
 LANES = 2 * BLK
 WIDE = 256
+LAG = 2
 
 
 def dct_table():
@@ -69,11 +70,83 @@
     return 8 if strips % 8 == 0 else strips
 
 
-def momentum_kernel(scale, strips, x_ref, g_ref, m_ref, sel_ref, table_ref, fresh_ref, sent_ref, acc_ref):
+def momentum_kernel(
+    axis, n, scale, strips, own_ref, x_ref, m_ref, w_ref, sel_ref, table_ref,
+    fresh_ref, sent_ref, dacts_ref, acc_ref, all_ref, dacts_acc, send_sem, recv_sem,
+):
+    me = lax.axis_index(axis)
+    right, left = lax.rem(me + 1, n), lax.rem(me + n - 1, n)
+    depth = own_ref.shape[0]
+    pieces = all_ref.shape[0] // 2
+    turn = pl.program_id(0)
+
+    def rows_of(owner):
+        return pl.ds(pl.multiple_of(owner * depth, depth), depth)
+
+    def hop(step, piece, way):
+        chunk = way * pieces + piece
+        owner = lax.rem(me + n - step, n) if way == 0 else lax.rem(me + step, n)
+        there = all_ref.at[chunk, rows_of(owner)]
+        return pltpu.make_async_remote_copy(
+            src_ref=own_ref.at[:, pl.ds(chunk * WIDE, WIDE)] if step == 0 else there,
+            dst_ref=there,
+            send_sem=send_sem.at[step, chunk],
+            recv_sem=recv_sem.at[step, chunk],
+            device_id={axis: right if way == 0 else left},
+            device_id_type=pl.DeviceIdType.MESH,
+        )
+
+    def forward(tick):
+        for step in reversed(range(n - 1)):
+            piece = tick - LAG * step
+            if 0 <= piece < pieces:
+                for way in range(2):
+                    if step > 0:
+                        hop(step - 1, piece, way).wait_recv()
+                    hop(step, piece, way).start()
+
+    ready = LAG * (n - 2) + 1
+
+    @pl.when(turn == 0)
+    def _():
+        barrier = pltpu.get_barrier_semaphore()
+        for peer in (left, right):
+            pl.semaphore_signal(barrier, inc=1, device_id={axis: peer}, device_id_type=pl.DeviceIdType.MESH)
+        pl.semaphore_wait(barrier, 2)
+        for tick in range(ready):
+            forward(tick)
+            if tick == 0:
+                for chunk in range(2 * pieces):
+                    all_ref[chunk, rows_of(me)] = own_ref[:, pl.ds(chunk * WIDE, WIDE)]
+                dacts_acc[...] = jnp.zeros_like(dacts_acc)
+
+    for piece in range(pieces):
+        @pl.when(turn == 2 * piece)
+        def _():
+            forward(piece + ready)
+            for way in range(2):
+                hop(n - 2, piece, way).wait_recv()
+
+    @pl.when(turn == 2 * pieces - 1)
+    def _():
+        for step in range(n - 1):
+            for piece in range(pieces):
+                for way in range(2):
+                    hop(step, piece, way).wait_send()
+
+    grads = all_ref[lax.rem(turn, 2) * pieces + turn // 2]
     acc_ref[...] = (
-        jnp.dot(x_ref[...], g_ref[...], preferred_element_type=jnp.float32) * scale
+        jnp.dot(x_ref[...], grads, preferred_element_type=jnp.float32) * scale
         + 0.999 * m_ref[...].astype(jnp.float32)
     )
+    dacts_acc[...] += lax.dot_general(
+        grads, w_ref[...], (((1,), (1,)), ((), ())), preferred_element_type=jnp.float32
+    )
+
+    @pl.when(turn == 2 * pieces - 1)
+    def _():
+        dacts_ref[...] = dacts_acc[...].astype(jnp.bfloat16)
+
     table = table_ref[...]
 
     some = group_of(strips)
@@ -122,30 +195,6 @@
         )
     pl.semaphore_wait(barrier, n - 1)
     return me
-
-
-def gather_kernel(axis, n, own_ref, all_ref, send_sem, recv_sem, own_sem):
-    me = greet(axis, n)
-    depth = own_ref.shape[0]
-    place = all_ref.at[pl.ds(pl.multiple_of(me * depth, depth), depth)]
-    copies = [
-        pltpu.make_async_remote_copy(
-            src_ref=own_ref,
-            dst_ref=place,
-            send_sem=send_sem.at[step],
-            recv_sem=recv_sem.at[step],
-            device_id={axis: lax.rem(me + step, n)},
-            device_id_type=pl.DeviceIdType.MESH,
-        )
-        for step in range(1, n)
-    ]
-    for copy in copies:
-        copy.start()
-    own = pltpu.make_async_copy(own_ref, place, own_sem)
-    own.start()
-    own.wait()
-    for copy in copies:
-        copy.wait()
 
 
 def mean_kernel(axis, n, sent_ref, mean_ref, parts, total, send_sem, recv_sem, back_sem, give_sem):
@@ -190,24 +239,6 @@
         copy.wait()
 
 
-def gather_rows(array, axis):
-    n = lax.axis_size(axis)
-    depth, cols = array.shape
-    return pl.pallas_call(
-        functools.partial(gather_kernel, axis, n),
-        out_shape=jax.ShapeDtypeStruct((n * depth, cols), array.dtype),
-        in_specs=[pl.BlockSpec(memory_space=pltpu.VMEM)],
-        out_specs=pl.BlockSpec(memory_space=pl.ANY),
-        scratch_shapes=[
-            pltpu.SemaphoreType.DMA((n,)),
-            pltpu.SemaphoreType.DMA((n,)),
-            pltpu.SemaphoreType.DMA,
-        ],
-        compiler_params=pltpu.CompilerParams(collective_id=0, has_side_effects=True),
-        name="gather_rows",
-    )(array)
-
-
 def mean_over(array, axis):
     n = lax.axis_size(axis)
     lanes = array.shape[-1]
@@ -234,38 +265,44 @@
     scale = 1.0 / math.sqrt(tokens)
     strips, steps = rows // BLK, cols // WIDE
     table = jnp.asarray(dct_table())
-    gathered = gather_rows(out_grad, "tensor")
+    n = lax.axis_size("tensor")
     turned = inputs.T
     picks = selected.reshape(strips, cols // LANES, LANES).swapaxes(0, 1)
 
     small = pl.BlockSpec((WIDE // LANES, strips, LANES), lambda c: (c, 0, 0))
     whole_table = pl.BlockSpec((BLK, LANES), lambda c: (0, 0))
     tall = pl.BlockSpec((rows, WIDE), lambda c: (0, c))
-    fresh, sent = pl.pallas_call(
-        functools.partial(momentum_kernel, scale, strips),
+    half = steps // 2
+    tall_turn = pl.BlockSpec((rows, WIDE), lambda c: (0, (c % 2) * half + c // 2))
+    small_turn = pl.BlockSpec((WIDE // LANES, strips, LANES), lambda c: ((c % 2) * half + c // 2, 0, 0))
+    fresh, sent, dacts = pl.pallas_call(
+        functools.partial(momentum_kernel, "tensor", n, scale, strips),
         grid=(steps,),
         out_shape=(
             jax.ShapeDtypeStruct((rows, cols), jnp.bfloat16),
             jax.ShapeDtypeStruct((cols // LANES, strips, LANES), jnp.float32),
+            jax.ShapeDtypeStruct((tokens, rows), jnp.bfloat16),
         ),
         in_specs=[
+            pl.BlockSpec(out_grad.shape, lambda c: (0, 0)),
             pl.BlockSpec((rows, tokens), lambda c: (0, 0)),
-            pl.BlockSpec((tokens, WIDE), lambda c: (0, c)),
-            tall,
-            small,
+            tall_turn,
+            tall_turn,
+            small_turn,
             whole_table,
         ],
-        out_specs=(tall, small),
-        scratch_shapes=[pltpu.VMEM((rows, WIDE), jnp.float32)],
-        cost_estimate=pl.CostEstimate(
-            flops=2 * rows * cols * (tokens + 512), bytes_accessed=8 * rows * cols, transcendentals=0
-        ),
+        out_specs=(tall_turn, small_turn, pl.BlockSpec((tokens, rows), lambda c: (0, 0))),
+        scratch_shapes=[
+            pltpu.VMEM((rows, WIDE), jnp.float32),
+            pltpu.VMEM((steps, tokens, WIDE), jnp.bfloat16),
+            pltpu.VMEM((tokens, rows), jnp.float32),
+            pltpu.SemaphoreType.DMA((n - 1, steps)),
+            pltpu.SemaphoreType.DMA((n - 1, steps)),
+        ],
+        compiler_params=pltpu.CompilerParams(collective_id=0, has_side_effects=True),
         name="momentum_step",
-    )(turned, gathered, momentum[0], picks, table)
+    )(out_grad, turned, momentum[0], weight, picks, table)
     mean_sent = mean_over(sent, "replica")
-    dacts = lax.dot_general(
-        gathered, weight, (((1,), (1,)), ((), ())), preferred_element_type=jnp.float32
-    ).astype(jnp.bfloat16)
     update = pl.pallas_call(
         functools.partial(update_kernel, strips),
         grid=(steps,),

time: 129 us -> 102 us (0.79)
  the two profiles are of different devices: /device:TPU:9 before, /device:TPU:0 now
where the time goes in v4:
time: 102 us
  Pallas kernels  90.8 us (89%)
  local copies, waits for them, and re-layouts  10.3 us (10%)
    pallas_call x1, Pallas kernels, body(): pl.pallas_call(functools.partial(momentum_kernel, 'tensor', n, scale, str...  61.1 us
    pallas_call x1, Pallas kernels, body(): pl.pallas_call(functools.partial(update_kernel, strips), grid=(steps,), o...  17.9 us
    pallas_call x1, Pallas kernels, mean_over(): pl.pallas_call(functools.partial(mean_kernel, axis, n), out_shape=jax.Sha...  11.8 us
    unnamed x6, local copies, waits for them, and re-layouts  9.51 us

profile of v4, /device:TPU:0, one launch (start us, length us, event | category | flops | bytes accessed | tf_op | source)
XLA Modules:
  0.0 101.8 jit_solution(1981068007255556316)
XLA Ops:
  0.6 1.1 %copy.11 = s32[640,64]{1,0:T(8,128)S(1)} copy(s32[640,64]{0,1:T(8,128)} %param.10) | data formatting | bytes 327680 | tf_op args[4]
  1.7 0.1 reshape.15
  1.8 0.7 copy.14
  2.5 2.3 %copy.10 = bf16[512,1024]{0,1:T(8,128)(2,1)} copy(bf16[512,1024]{1,0:T(8,128)(2,1)} %param.6) | data formatting | bytes 2097152 | tf_op args[0]
  4.8 61.1 %momentum_step.1 = (bf16[1024,2560]{1,0:T(8,128)(2,1)}, f32[20,16,128]{2,1,0:T(8,128)}, bf16[512,1024]{1,0:T(8,128)(2,1)}) custom-call(bf16[128,2560]{1,0:T(8,128)(2,1)} %own_ref.1, bf16[1024,512]{1,0:T(8,128)(2,1)} %bitcast.10, bf16[1024,2560]{1,0:T(8,128)(2,1)} %bitcast.8, bf16[1024,2560]{1,0:T(8,128)(2,1)} %w_ref.1, s32[20,16,128]{2,1,0:T(8,128)} %bitcast.11, ...), custom_call_target="tpu_custom_call" | custom-call | tf_op jit(solution)/shard_map/momentum_step/pallas_call | solution.py:278
  65.9 0.0 copy-start
  65.9 11.8 %mean_over.1 = f32[8,40,128]{2,1,0:T(8,128)} custom-call(f32[8,40,128]{2,1,0:T(8,128)} %bitcast.14), custom_call_target="tpu_custom_call" | custom-call | tf_op jit(solution)/shard_map/mean_over/pallas_call | solution.py:246
  77.7 17.9 %update_step.1 = bf16[1024,2560]{1,0:T(8,128)(2,1)} custom-call(f32[20,16,128]{2,1,0:T(8,128)} %bitcast.13, s32[20,16,128]{2,1,0:T(8,128)} %bitcast.12, f32[64,128]{1,0:T(8,128)} %constant.2.clone.table_ref), custom_call_target="tpu_custom_call" | custom-call | flops 1342177280 | bytes 5242880 | tf_op jit(solution)/shard_map/update_step/pallas_call | solution.py:306
  95.6 0.0 copy-done
  95.6 1.0 copy.17
  96.6 5.2 %copy.18 = bf16[1,1024,2560]{2,1,0:T(8,128)(2,1)} copy(bf16[1,1024,2560]{2,1,0:T(8,128)(2,1)} %bitcast.9) | data formatting | bytes 10485760
Async XLA Ops:
  65.9 29.8 %copy-start = (bf16[512,1024]{1,0:T(8,128)(2,1)S(1)}, bf16[512,1024]{1,0:T(8,128)(2,1)}, u32[]{:S(2)}) copy-start(bf16[512,1024]{1,0:T(8,128)(2,1)} %get-tuple-element.12) | copy-start | bytes 3145732

commit v5 on v4

--- a/solution.py
+++ b/solution.py
@@ -168,7 +168,8 @@
             sent_ref[pair, near] = jnp.concatenate(found, axis=0)
 
 
-def update_kernel(strips, mean_ref, sel_ref, table_ref, update_ref):
+def update_kernel(strips, mean_ref, sel_ref, table_ref, held_ref, update_ref, fresh_ref):
+    fresh_ref[...] = held_ref[...]
     table = table_ref[...]
 
     some = group_of(strips)
@@ -303,17 +304,17 @@
         name="momentum_step",
     )(out_grad, turned, momentum[0], weight, picks, table)
     mean_sent = mean_over(sent, "replica")
-    update = pl.pallas_call(
+    update, fresh = pl.pallas_call(
         functools.partial(update_kernel, strips),
         grid=(steps,),
-        out_shape=jax.ShapeDtypeStruct((rows, cols), jnp.bfloat16),
-        in_specs=[small, small, whole_table],
-        out_specs=tall,
+        out_shape=(jax.ShapeDtypeStruct((rows, cols), jnp.bfloat16),) * 2,
+        in_specs=[small, small, whole_table, tall],
+        out_specs=(tall, tall),
         cost_estimate=pl.CostEstimate(
             flops=2 * rows * cols * 256, bytes_accessed=2 * rows * cols, transcendentals=0
         ),
         name="update_step",
-    )(mean_sent, picks, table)
+    )(mean_sent, picks, table, fresh)
     return dacts, fresh[None], update
 
 

time: 102 us -> 97.7 us (0.958)
  local copies, waits for them, and re-layouts: 10.3 us -> 5.13 us
    unnamed x6 -> x5, local copies, waits for them, and re-layouts: 9.51 us -> 4.33 us
where the time goes in v5:
time: 97.7 us; the launch traced here: 97.5 us
  Pallas kernels  91.7 us (94%)
  local copies, waits for them, and re-layouts  5.13 us (5%)
    pallas_call x1, Pallas kernels, body(): pl.pallas_call(functools.partial(momentum_kernel, 'tensor', n, scale, str...  61.1 us
    pallas_call x1, Pallas kernels, body(): pl.pallas_call(functools.partial(update_kernel, strips), grid=(steps,), o...  18.8 us
    pallas_call x1, Pallas kernels, mean_over(): pl.pallas_call(functools.partial(mean_kernel, axis, n), out_shape=jax.Sha...  11.8 us
    unnamed x5, local copies, waits for them, and re-layouts  4.33 us

profile of v5, /device:TPU:0, one launch (start us, length us, event | category | flops | bytes accessed | tf_op | source)
XLA Modules:
  0.0 97.5 jit_solution(11701713388916115971)
XLA Ops:
  0.6 1.1 %copy.11 = s32[640,64]{1,0:T(8,128)S(1)} copy(s32[640,64]{0,1:T(8,128)} %param.10) | data formatting | bytes 327680 | tf_op args[4]
  1.7 0.1 reshape.15
  1.8 0.7 copy.14
  2.5 2.3 %copy.10 = bf16[512,1024]{0,1:T(8,128)(2,1)} copy(bf16[512,1024]{1,0:T(8,128)(2,1)} %param.6) | data formatting | bytes 2097152 | tf_op args[0]
  4.8 61.1 %momentum_step.1 = (bf16[1024,2560]{1,0:T(8,128)(2,1)}, f32[20,16,128]{2,1,0:T(8,128)}, bf16[512,1024]{1,0:T(8,128)(2,1)}) custom-call(bf16[128,2560]{1,0:T(8,128)(2,1)} %own_ref.1, bf16[1024,512]{1,0:T(8,128)(2,1)} %bitcast.9, bf16[1024,2560]{1,0:T(8,128)(2,1)} %bitcast.8, bf16[1024,2560]{1,0:T(8,128)(2,1)} %w_ref.1, s32[20,16,128]{2,1,0:T(8,128)} %bitcast.10, ...), custom_call_target="tpu_custom_call" | custom-call | tf_op jit(solution)/shard_map/momentum_step/pallas_call | solution.py:279
  65.9 0.0 copy-start
  65.9 11.8 %mean_over.1 = f32[8,40,128]{2,1,0:T(8,128)} custom-call(f32[8,40,128]{2,1,0:T(8,128)} %bitcast.13), custom_call_target="tpu_custom_call" | custom-call | tf_op jit(solution)/shard_map/mean_over/pallas_call | solution.py:247
  77.7 18.8 %update_step.1 = (bf16[1024,2560]{1,0:T(8,128)(2,1)}, bf16[1024,2560]{1,0:T(8,128)(2,1)}) custom-call(f32[20,16,128]{2,1,0:T(8,128)} %bitcast.12, s32[20,16,128]{2,1,0:T(8,128)} %bitcast.11, f32[64,128]{1,0:T(8,128)} %constant.2.clone.table_ref, bf16[1024,2560]{1,0:T(8,128)(2,1)} %get-tuple-element.10.held_ref), custom_call_target="tpu_custom_call" | custom-call | flops 1342177280 | bytes 5242880 | tf_op jit(solution)/shard_map/update_step/pallas_call | solution.py:307
  96.5 0.0 copy-done
  96.5 1.0 copy.16
Async XLA Ops:
  65.9 30.6 %copy-start = (bf16[512,1024]{1,0:T(8,128)(2,1)S(1)}, bf16[512,1024]{1,0:T(8,128)(2,1)}, u32[]{:S(2)}) copy-start(bf16[512,1024]{1,0:T(8,128)(2,1)} %get-tuple-element.16) | copy-start | bytes 3145732
